TPU v7x, 32 devices: a whole 2x2x4 slice. The times are simulated.
32 devices in a mesh: loop: 8 (over y, x, core), tp: 4 (over z).
Axes of the slice: x: 2, y: 2, z: 4, core: 2. Of those that a mesh axis runs over, the one named last changes fastest.
Arguments:
- tokens: bfloat16 [2048, 4096], P('loop', 'tp'), may hold values from -6 to 6
- out_grad: bfloat16 [2048, 6144], P('loop', 'tp'), may hold values from -6 to 6
- qkv_weight: bfloat16 [3, 4096, 6144], P(None, 'loop', 'tp'), may hold values from -0.09375 to 0.09375
- dest_row: int32 [2048], P('loop'), may hold values from 0 to 383, as said below
- loop_modality: int32 [8], replicated, may hold values from 0 to 2, as said below
Outputs:
- projected: bfloat16 [2048, 6144], P('loop', 'tp')
- input_grad: bfloat16 [2048, 4096], P('loop', 'tp')
- weight_grad: bfloat16 [3, 4096, 6144], P(None, 'loop', 'tp')
Inputs may be any that keep to these rules, and one draw needn't show every extreme that they name: `dest_row`: within each aligned block of 256 tokens the values are distinct, so at most 48 tokens of one block name one loop; in every draw some loop is named by exactly 48 tokens of every block. `loop_modality`: A quarter of the loops hold 0, half hold 1, a quarter hold 2.
All inputs are finite; a program needn't handle non-finite values.
Results may differ from a plain program's by a relative error of at most 0.014.
Values may be sent and summed in bfloat16 or wider, within the bound.
No kernel may reach another device: no remote copies, remote signals or barrier semaphores. Data moves between devices by JAX's collectives and lax.ppermute only.
A program may use at most 128 MiB of HBM per device.

v0:
```python
import math
import jax
import jax.numpy as jnp
from jax import lax
from jax.sharding import PartitionSpec as P


def per_device(tokens, out_grad, qkv_weight, dest_row, loop_modality):
    loop_count = lax.axis_size("loop")
    row_count, feature_part = tokens.shape
    kinds, block_rows, column_count = qkv_weight.shape
    capacity = 3 * row_count // (2 * loop_count)
    grad_scale = 1.0 / math.sqrt(row_count * loop_count)
    own_kind = loop_modality[dest_row // capacity]
    kind_of = lax.all_gather(own_kind, "loop", axis=0, tiled=True)
    grads = lax.all_gather(out_grad, "loop", axis=0, tiled=True)
    features = lax.all_gather(tokens, "tp", axis=1, tiled=True)
    rows = lax.all_to_all(features, "loop", split_axis=1, concat_axis=0, tiled=True)
    masks = [(kind_of == kind)[:, None] for kind in range(kinds)]
    term = sum(
        (
            lax.dot_general(
                jnp.where(masks[kind], grads, 0),
                qkv_weight[kind],
                (((1,), (1,)), ((), ())),
                preferred_element_type=jnp.float32,
            )
            for kind in range(kinds)
        )
    ).astype(jnp.bfloat16)
    term = lax.all_to_all(term, "loop", split_axis=0, concat_axis=1, tiled=True)
    input_grad = lax.psum_scatter(term, "tp", scatter_dimension=1, tiled=True)
    partial = sum(
        (
            jnp.dot(
                jnp.where(masks[kind], rows, 0),
                qkv_weight[kind],
                preferred_element_type=jnp.float32,
            )
            for kind in range(kinds)
        )
    ).astype(jnp.bfloat16)
    projected = lax.psum_scatter(partial, "loop", scatter_dimension=0, tiled=True)
    weight_grad = jnp.stack(
        [
            (
                lax.dot_general(
                    jnp.where(masks[kind], rows, 0),
                    grads,
                    (((0,), (0,)), ((), ())),
                    preferred_element_type=jnp.float32,
                )
                * grad_scale
            ).astype(jnp.bfloat16)
            for kind in range(kinds)
        ]
    )
    return (projected, input_grad, weight_grad)


def solution(mesh):
    placed = (P("loop", "tp"), P("loop", "tp"), P(None, "loop", "tp"), P("loop"), P())
    return jax.shard_map(
        per_device,
        mesh=mesh,
        in_specs=placed,
        out_specs=(P("loop", "tp"), P("loop", "tp"), P(None, "loop", "tp")),
        check_vma=False,
    )
```

profile of v0, /device:TPU:0, one launch (start us, length us, event | category | flops | bytes accessed | tf_op | source)
XLA Modules:
  0.0 278.5 jit_solution(15667492491029857206)
XLA Ops:
  7.2 0.0 copy-start.2
  7.2 0.0 copy-start.3
  7.2 0.0 all-gather.5.cloned.1.call-start
  7.2 2.0 copy.17
  9.3 0.0 all-gather.5.cloned.1.call-update
  9.3 0.0 all-gather.7.cloned.1.call-start
  9.3 0.7 all-gather.7.cloned.1.call-update
  10.0 48.5 %all-gather.5.cloned.1.call-done = bf16[256,4096]{0,1:T(8,128)(2,1)} async-done(((bf16[256,1024]{0,1:T(8,128)(2,1)}), bf16[256,4096]{0,1:T(8,128)(2,1)}) %all-gather.5.cloned.1.call-update) | async-done | bytes 2097168 | tf_op jit(solution)/shard_map/all_gather | solution.py:17
  58.5 3.7 %all-to-all-start = ((bf16[256,8,512]{0,2,1:T(8,128)(2,1)}), bf16[256,8,512]{0,2,1:T(8,128)(2,1)S(1)}, u32[]{:S(2)}, u32[]{:S(2)}) async-start(bf16[256,8,512]{0,2,1:T(8,128)(2,1)} %bitcast.68), calls=%async_computation | async-start | bytes 4194304 | tf_op jit(solution)/shard_map/all_to_all | solution.py:18
  62.2 0.0 reduce-scatter.3.cloned.1.call-start
  62.2 0.0 copy-done.2
  62.3 0.7 fusion.37
  62.9 0.0 copy-done.3
  63.0 5.2 %compare_select_fusion.1 = s32[256]{0:T(256)S(1)} fusion(s32[256]{0:T(256)S(1)} %copy-done.3, s32[]{:T(128)} %bitcast, s32[]{:T(128)} %bitcast.1, s32[]{:T(128)} %bitcast.2, s32[]{:T(128)} %bitcast.3, s32[]{:T(128)} %bitcast.4, s32[]{:T(128)} %bitcast.5, s32[]{:T(128)} %bitcast.6, s32[]{:T(128)} %bitcast.7), kind=kLoop, calls=%fused_computation.48 | loop fusion | flops 6400 | bytes 2080 | tf_op jit(solution)/shard_map/gather | solution.py:14
  68.1 32.2 %all-gather.1 = s32[8,1,256]{2,1,0:T(1,128)S(1)} all-gather(s32[1,1,256]{2,1,0:T(1,128)S(1)} %bitcast.75), channel_id=2, replica_groups=mesh['loop'=8,'tp'=4] {'loop'}, dimensions={0}, use_global_device_ids=true | all-gather | bytes 9216 | tf_op jit(solution)/shard_map/all_gather | solution.py:15
  100.3 0.0 all-to-all-done
  100.3 2.8 %broadcast_select_fusion = (bf16[8,256,512]{1,2,0:T(8,128)(2,1)}, bf16[8,256,512]{1,2,0:T(8,128)(2,1)}, bf16[8,256,512]{1,2,0:T(8,128)(2,1)}) fusion(pred[8,256]{1,0:T(8,128)(4,1)S(1)} %bitcast.72, bf16[256,8,512]{0,2,1:T(8,128)(2,1)S(1)} %all-to-all-done, pred[8,256]{1,0:T(8,128)(4,1)S(1)} %bitcast.74, pred[8,256]{1,0:T(8,128)(4,1)S(1)} %bitcast.73), kind=kLoop, calls=%fused_computation.27 | loop fusion | flops 3145728 | bytes 8394752 | tf_op jit(solution)/shard_map/jit(_where)/select_n | solution.py:36
  103.2 3.9 %copy.20 = bf16[8,256,512]{2,1,0:T(8,128)(2,1)} copy(bf16[8,256,512]{1,2,0:T(8,128)(2,1)} %get-tuple-element.8) | data formatting | bytes 4194304 | tf_op jit(solution)/shard_map/jit(_where)/select_n | solution.py:36
  107.1 4.0 %copy.18 = bf16[8,256,512]{2,1,0:T(8,128)(2,1)} copy(bf16[8,256,512]{1,2,0:T(8,128)(2,1)} %get-tuple-element.7) | data formatting | bytes 4194304 | tf_op jit(solution)/shard_map/jit(_where)/select_n | solution.py:36
  111.1 3.9 %copy.22 = bf16[8,256,512]{2,1,0:T(8,128)(2,1)} copy(bf16[8,256,512]{1,2,0:T(8,128)(2,1)} %get-tuple-element.6) | data formatting | bytes 4194304 | tf_op jit(solution)/shard_map/jit(_where)/select_n | solution.py:36
  115.0 0.0 copy-start.1
  115.0 10.2 %fusion.23 = f32[2048,1536]{1,0:T(8,128)} fusion(bf16[2048,512]{1,0:T(8,128)(2,1)} %bitcast.69, bf16[3,512,1536]{2,1,0:T(8,128)(2,1)} %param.7), kind=kOutput, calls=%fused_computation.33 | convolution fusion | flops 3221225472 | bytes 16252928 | tf_op jit(solution)/shard_map/dot_general | solution.py:35
  125.2 0.0 copy-done.1
  125.2 0.0 copy-start
  125.2 7.8 %fusion.26 = f32[2048,1536]{1,0:T(8,128)} fusion(bf16[2048,512]{1,0:T(8,128)(2,1)S(1)} %bitcast.70, bf16[3,512,1536]{2,1,0:T(8,128)(2,1)} %param.7), kind=kOutput, calls=%fused_computation.36 | convolution fusion | flops 3221225472 | bytes 16252928 | tf_op jit(solution)/shard_map/dot_general | solution.py:35
  133.0 0.0 copy-done
  133.0 13.3 %add_convert_fusion = bf16[2048,1536]{1,0:T(8,128)(2,1)} fusion(f32[2048,1536]{1,0:T(8,128)} %fusion.26, f32[2048,1536]{1,0:T(8,128)} %fusion.23, bf16[2048,512]{1,0:T(8,128)(2,1)S(1)} %bitcast.65, bf16[3,512,1536]{2,1,0:T(8,128)(2,1)} %param.7), kind=kOutput, calls=%fused_computation | convolution fusion | flops 3230662656 | bytes 35127296 | tf_op jit(solution)/shard_map/dot_general | solution.py:35
  146.3 0.0 reduce-scatter.3.cloned.1.call-update
  146.4 0.2 reduce-scatter.5.cloned.1.call-start
  146.6 0.0 all-gather.7.cloned.1.call-done
  146.7 0.0 copy-start.4
  146.7 6.3 %fusion = f32[2048,512]{1,0:T(8,128)S(1)} fusion(bf16[2048,1536]{1,0:T(8,128)(2,1)} %all-gather.7.cloned.1.call-done, pred[2048]{0:T(1024)(128)(4,1)S(1)} %reshape.57, bf16[3,512,1536]{2,1,0:T(8,128)(2,1)} %param.7), kind=kOutput, calls=%fused_computation.1 | convolution fusion | flops 3224371200 | bytes 12060672 | tf_op jit(solution)/shard_map/dot_general | solution.py:22
  153.0 0.0 copy-done.4
  153.0 5.2 %fusion.2 = f32[2048,512]{1,0:T(8,128)S(1)} fusion(bf16[2048,1536]{1,0:T(8,128)(2,1)S(1)} %copy-done.4, pred[2048]{0:T(1024)(128)(4,1)S(1)} %reshape.55, bf16[3,512,1536]{2,1,0:T(8,128)(2,1)} %param.7), kind=kOutput, calls=%fused_computation.3 | convolution fusion | flops 3224371200 | bytes 12060672 | tf_op jit(solution)/shard_map/dot_general | solution.py:22
  158.2 5.2 %add_convert_fusion.1 = bf16[2048,512]{1,0:T(8,128)(2,1)S(1)} fusion(f32[2048,512]{1,0:T(8,128)S(1)} %fusion, f32[2048,512]{1,0:T(8,128)S(1)} %fusion.2, bf16[2048,1536]{1,0:T(8,128)(2,1)S(1)} %copy-done.4, pred[2048]{0:T(1024)(128)(4,1)S(1)} %reshape.53, bf16[3,512,1536]{2,1,0:T(8,128)(2,1)} %param.7), kind=kOutput, calls=%fused_computation.11 | convolution fusion | flops 3227516928 | bytes 18352128 | tf_op jit(solution)/shard_map/dot_general | solution.py:22
  163.4 45.9 %all_to_all.38 = bf16[8,256,512]{2,1,0:T(8,128)(2,1)S(1)} all-to-all(bf16[8,256,512]{2,1,0:T(8,128)(2,1)S(1)} %bitcast.71), channel_id=1, replica_groups=mesh['loop'=8,'tp'=4] {'loop'}, dimensions={0} | all-to-all | bytes 4194304 | tf_op jit(solution)/shard_map/all_to_all | solution.py:31
  209.3 1.6 copy.25
  210.9 0.0 reduce-scatter.5.cloned.1.call-update
  210.9 2.4 copy.24
  213.3 3.7 %bitcast_select_fusion.2 = (bf16[2048,512]{1,0:T(8,128)(2,1)S(1)}, bf16[2048,512]{1,0:T(8,128)(2,1)S(1)}, bf16[2048,512]{1,0:T(8,128)(2,1)S(1)}) fusion(bf16[8,256,512]{2,1,0:T(8,128)(2,1)} %copy.24, pred[2048]{0:T(1024)(128)(4,1)S(1)} %reshape.53, pred[2048]{0:T(1024)(128)(4,1)S(1)} %reshape.55, pred[2048]{0:T(1024)(128)(4,1)S(1)} %reshape.57), kind=kLoop, calls=%fused_computation.26 | loop fusion | flops 3145728 | bytes 8394752 | tf_op jit(solution)/shard_map/jit(_where)/select_n | solution.py:36
  217.0 0.0 slice-start.1
  217.0 6.5 %fusion.15 = bf16[1,512,1536]{2,1,0:T(8,128)(2,1)S(1)} fusion(bf16[2048,512]{1,0:T(8,128)(2,1)S(1)} %get-tuple-element.5, bf16[2048,1536]{1,0:T(8,128)(2,1)} %all-gather.7.cloned.1.call-done), kind=kOutput, calls=%fused_computation.21 | convolution fusion | flops 3222798336 | bytes 9961472 | tf_op jit(solution)/shard_map/dot_general | solution.py:47
  223.5 0.0 slice-done
  223.5 0.0 slice-done.1
  223.5 3.6 %fusion.16 = bf16[1,512,1536]{2,1,0:T(8,128)(2,1)S(1)} fusion(bf16[2048,512]{1,0:T(8,128)(2,1)S(1)} %get-tuple-element.4, bf16[2048,1536]{1,0:T(8,128)(2,1)S(1)} %bitcast.77), kind=kOutput, calls=%fused_computation.22 | convolution fusion | flops 3222798336 | bytes 9961472 | tf_op jit(solution)/shard_map/dot_general | solution.py:47
  227.1 3.6 %fusion.17 = bf16[1,512,1536]{2,1,0:T(8,128)(2,1)S(1)} fusion(bf16[2048,512]{1,0:T(8,128)(2,1)S(1)} %get-tuple-element.3, bf16[2048,1536]{1,0:T(8,128)(2,1)S(1)} %bitcast.77), kind=kOutput, calls=%fused_computation.23 | convolution fusion | flops 3222798336 | bytes 9961472 | tf_op jit(solution)/shard_map/dot_general | solution.py:47
  230.7 2.5 pad_maximum_fusion
  233.2 38.8 %reduce-scatter.5.cloned.1.call-done = bf16[256,1024]{1,0:T(8,128)(2,1)} async-done(((bf16[256,4096]{1,0:T(8,128)(2,1)}), bf16[256,1024]{1,0:T(8,128)(2,1)}) %reduce-scatter.5.cloned.1.call-update) | async-done | bytes 524304 | tf_op jit(solution)/shard_map/reduce_scatter | solution.py:32
  (7 shorter events, 0.0 us)
Async XLA Ops:
  7.2 55.1 %copy-start.2 = (s32[8]{0:T(128)S(1)}, s32[8]{0:T(128)}, u32[]{:S(2)}) copy-start(s32[8]{0:T(128)} %param.9) | copy-start | bytes 100
  7.2 55.8 %copy-start.3 = (s32[256]{0:T(256)S(1)}, s32[256]{0:T(256)}, u32[]{:S(2)}) copy-start(s32[256]{0:T(256)} %param.8) | copy-start | bytes 3076
  7.2 51.4 %all-gather.5.cloned.1.call-start = ((), (), s32[]{:S(2)}) async-start(), calls=%async_computation.4 | async-start | bytes 2621440 | tf_op jit(solution)/shard_map/all_gather | solution.py:17
  9.3 137.4 %all-gather.7.cloned.1.call-start = ((), (), s32[]{:S(2)}) async-start(), calls=%async_computation.6 | async-start | bytes 7077888 | tf_op jit(solution)/shard_map/all_gather | solution.py:16
  58.5 41.8 %all-to-all-start = ((bf16[256,8,512]{0,2,1:T(8,128)(2,1)}), bf16[256,8,512]{0,2,1:T(8,128)(2,1)S(1)}, u32[]{:S(2)}, u32[]{:S(2)}) async-start(bf16[256,8,512]{0,2,1:T(8,128)(2,1)} %bitcast.68), calls=%async_computation | async-start | bytes 4194304 | tf_op jit(solution)/shard_map/all_to_all | solution.py:18
  62.2 171.0 %reduce-scatter.3.cloned.1.call-start = ((), (), s32[]{:S(2)}) async-start(), calls=%async_computation.5 | async-start | bytes 7077888 | tf_op jit(solution)/shard_map/reduce_scatter | solution.py:43
  115.0 10.2 %copy-start.1 = (bf16[8,256,512]{2,1,0:T(8,128)(2,1)S(1)}, bf16[8,256,512]{2,1,0:T(8,128)(2,1)}, u32[]{:S(2)}) copy-start(bf16[8,256,512]{2,1,0:T(8,128)(2,1)} %copy.18) | copy-start | bytes 6291460
  125.2 7.9 %copy-start = (bf16[8,256,512]{2,1,0:T(8,128)(2,1)S(1)}, bf16[8,256,512]{2,1,0:T(8,128)(2,1)}, u32[]{:S(2)}) copy-start(bf16[8,256,512]{2,1,0:T(8,128)(2,1)} %copy.22) | copy-start | bytes 6291460
  146.4 125.6 %reduce-scatter.5.cloned.1.call-start = ((), (), s32[]{:S(2)}) async-start(), calls=%async_computation.7 | async-start | bytes 2621440 | tf_op jit(solution)/shard_map/reduce_scatter | solution.py:32
  146.7 6.3 %copy-start.4 = (bf16[2048,1536]{1,0:T(8,128)(2,1)S(1)}, bf16[2048,1536]{1,0:T(8,128)(2,1)}, u32[]{:S(2)}) copy-start(bf16[2048,1536]{1,0:T(8,128)(2,1)} %all-gather.7.cloned.1.call-done) | copy-start | bytes 18874372
  213.3 10.2 %slice-start = ((s8[6291456]{0:T(1024)(128)(4,1)}), s8[4194304]{0:T(1024)(128)(4,1)S(1)}, s32[]{:S(2)}) async-start(s8[6291456]{0:T(1024)(128)(4,1)} %bitcast.76), calls=%async_computation.8 | async-start | bytes 8388608
  217.0 6.5 %slice-start.1 = ((s8[6291456]{0:T(1024)(128)(4,1)}), s8[2097152]{0:T(1024)(128)(4,1)S(1)}, s32[]{:S(2)}) async-start(s8[6291456]{0:T(1024)(128)(4,1)} %bitcast.76), calls=%async_computation.9 | async-start | bytes 4194304
Sparse Core Ops, SparseCore 0:
  10.1 48.3 all-gather.4
  60.4 58.3 all-gather.6
  146.5 79.0 reduce-scatter.2
  228.3 43.6 reduce-scatter.4
where the time goes:
time: 279 us
  waiting for transfers between devices  88.1 us (32%)
  blocking collectives  78.1 us (28%)
  matrix products  61.7 us (22%)
  local copies, waits for them, and re-layouts  18.6 us (7%)
  other arithmetic  14.1 us (5%)
  between operations  13.9 us (5%)
  starting transfers between devices  3.99 us (1%)
    all_gather x1, waiting for transfers between devices, per_device(): features = lax.all_gather(tokens, 'tp', axis=1, tiled=True)  48.5 us
    all_to_all x1, blocking collectives, per_device(): term = lax.all_to_all(term, 'loop', split_axis=0, concat_axis=1, tiled=True)  45.9 us
    reduce_scatter x1, waiting for transfers between devices, per_device(): input_grad = lax.psum_scatter(term, 'tp', scatter_dimension=1, tiled=True)  38.8 us
    all_gather x1, blocking collectives, per_device(): kind_of = lax.all_gather(own_kind, 'loop', axis=0, tiled=True)  32.2 us
    dot_general x3, matrix products, per_device(): jnp.dot(jnp.where(masks[kind], rows, 0), qkv_weight[kind], preferred_elem...  31.3 us
    dot_general x3, matrix products, per_device(): lax.dot_general(jnp.where(masks[kind], grads, 0), qkv_weight[kind], (((1,...  16.7 us
    dot_general x3, matrix products, per_device(): lax.dot_general(jnp.where(masks[kind], rows, 0), grads, (((0,), (0,)), ((...  13.6 us
    select_n x3, local copies, waits for them, and re-layouts, per_device(): jnp.where(masks[kind], rows, 0)  11.8 us
  transfers between devices with their start and end apart: 5, of which 2 were waited for; matrix products, arithmetic and copies ran while one was open for 33% of the time, Pallas kernels for 0%

commit v1 on v0

--- a/solution.py
+++ b/solution.py
@@ -28,7 +28,10 @@
             for kind in range(kinds)
         )
     ).astype(jnp.bfloat16)
-    term = lax.all_to_all(term, "loop", split_axis=0, concat_axis=1, tiled=True)
+    term = jnp.concatenate(
+        lax.all_to_all(jnp.stack(jnp.split(term, lax.axis_size("loop"), axis=0)), "loop", 0, 0),
+        axis=1,
+    )
     input_grad = lax.psum_scatter(term, "tp", scatter_dimension=1, tiled=True)
     partial = sum(
         (

time: 279 us -> 256 us (0.918)
  blocking collectives: 78.1 us -> 10.6 us
  waiting for transfers between devices: 88.1 us -> 116 us
  local copies, waits for them, and re-layouts: 18.6 us -> 30.2 us
  starting transfers between devices: 3.99 us -> 7.55 us
    all_to_all x1 -> x0, blocking collectives: 45.9 us -> none  [per_device(): term = lax.all_to_all(term, 'loop', split_axis=0, concat_axis=1, tiled=True)]
    reduce_scatter x1, waiting for transfers between devices: 38.8 us -> 0.01 us  [per_device(): input_grad = lax.psum_scatter(term, 'tp', scatter_dimension=1, tiled=True)]
    reduce_scatter x1, waiting for transfers between devices: 0.01 us -> 35.2 us  [per_device(): lax.psum_scatter(partial, 'loop', scatter_dimension=0, tiled=True)]
    all_gather x1, waiting for transfers between devices: 0.02 us -> 31.5 us  [per_device(): grads = lax.all_gather(out_grad, 'loop', axis=0, tiled=True)]
    all_gather x1, waiting for transfers between devices: 48.5 us -> 22 us  [per_device(): features = lax.all_gather(tokens, 'tp', axis=1, tiled=True)]
    all_to_all x1, waiting for transfers between devices: 0.01 us -> 22.3 us  [per_device(): lax.all_to_all(features, 'loop', split_axis=1, concat_axis=0, tiled=True)]
    all_gather x1, blocking collectives: 32.2 us -> 10.6 us  [per_device(): kind_of = lax.all_gather(own_kind, 'loop', axis=0, tiled=True)]
    unnamed x15 -> x25, local copies, waits for them, and re-layouts: 2.07 us -> 10.6 us
  transfers between devices with their start and end apart: 5 -> 6, of which waited for: 2 -> 5; matrix products, arithmetic and copies ran while one was open for 33% -> 41% of each run, Pallas kernels for 0% -> 0%
where the time goes in v1:
time: 256 us; the launch traced here: 255 us
  waiting for transfers between devices  116 us (45%)
  matrix products  62.2 us (24%)
  local copies, waits for them, and re-layouts  30.2 us (12%)
  other arithmetic  14.7 us (6%)
  between operations  13.9 us (5%)
  blocking collectives  10.6 us (4%)
  starting transfers between devices  7.55 us (3%)
    reduce_scatter x1, waiting for transfers between devices, per_device(): lax.psum_scatter(partial, 'loop', scatter_dimension=0, tiled=True)  35.2 us
    all_gather x1, waiting for transfers between devices, per_device(): grads = lax.all_gather(out_grad, 'loop', axis=0, tiled=True)  31.5 us
    dot_general x3, matrix products, per_device(): jnp.dot(jnp.where(masks[kind], rows, 0), qkv_weight[kind], preferred_elem...  31.3 us
    all_to_all x1, waiting for transfers between devices, per_device(): lax.all_to_all(features, 'loop', split_axis=1, concat_axis=0, tiled=True)  22.3 us
    all_gather x1, waiting for transfers between devices, per_device(): features = lax.all_gather(tokens, 'tp', axis=1, tiled=True)  22 us
    dot_general x3, matrix products, per_device(): lax.dot_general(jnp.where(masks[kind], grads, 0), qkv_weight[kind], (((1,...  16.4 us
    dot_general x3, matrix products, per_device(): lax.dot_general(jnp.where(masks[kind], rows, 0), grads, (((0,), (0,)), ((...  14.6 us
    select_n x3, local copies, waits for them, and re-layouts, per_device(): jnp.where(masks[kind], rows, 0)  11.8 us
  transfers between devices with their start and end apart: 6, of which 5 were waited for; matrix products, arithmetic and copies ran while one was open for 41% of the time, Pallas kernels for 0%

profile of v1, /device:TPU:0, one launch (start us, length us, event | category | flops | bytes accessed | tf_op | source)
XLA Modules:
  0.0 255.5 jit_solution(1909891860356894327)
XLA Ops:
  7.2 0.0 all-gather.7.cloned.1.call-start
  7.2 0.7 all-gather.7.cloned.1.call-update
  7.9 0.0 all-gather.5.cloned.1.call-start
  8.0 2.0 copy.18
  10.0 0.0 all-gather.5.cloned.1.call-update
  10.0 0.7 fusion.45
  10.7 5.2 %compare_select_fusion.1 = s32[256]{0:T(256)S(1)} fusion(s32[256]{0:T(256)S(1)} %copy-done.4, s32[]{:T(128)} %bitcast, s32[]{:T(128)} %bitcast.1, s32[]{:T(128)} %bitcast.2, s32[]{:T(128)} %bitcast.3, s32[]{:T(128)} %bitcast.4, s32[]{:T(128)} %bitcast.5, s32[]{:T(128)} %bitcast.6, s32[]{:T(128)} %bitcast.7), kind=kLoop, calls=%fused_computation.64 | loop fusion | flops 6400 | bytes 2080 | tf_op jit(solution)/shard_map/gather | solution.py:14
  15.9 10.6 %all-gather.1 = s32[8,1,256]{2,1,0:T(1,128)S(1)} all-gather(s32[1,1,256]{2,1,0:T(1,128)S(1)} %bitcast.104), channel_id=2, replica_groups=mesh['loop'=8,'tp'=4] {'loop'}, dimensions={0}, use_global_device_ids=true | all-gather | bytes 9216 | tf_op jit(solution)/shard_map/all_gather | solution.py:15
  26.6 31.5 %all-gather.7.cloned.1.call-done = bf16[2048,1536]{1,0:T(8,128)(2,1)} async-done(((bf16[256,1536]{1,0:T(8,128)(2,1)}), bf16[2048,1536]{1,0:T(8,128)(2,1)}) %all-gather.7.cloned.1.call-update) | async-done | bytes 6291472 | tf_op jit(solution)/shard_map/all_gather | solution.py:16
  58.0 6.3 %fusion = f32[2048,512]{1,0:T(8,128)S(1)} fusion(bf16[2048,1536]{1,0:T(8,128)(2,1)} %all-gather.7.cloned.1.call-done, pred[2048]{0:T(1024)(128)(4,1)S(1)} %reshape.62, bf16[3,512,1536]{2,1,0:T(8,128)(2,1)} %param.7), kind=kOutput, calls=%fused_computation.1 | convolution fusion | flops 3224371200 | bytes 12060672 | tf_op jit(solution)/shard_map/dot_general | solution.py:22
  64.3 5.0 %fusion.2 = f32[2048,512]{1,0:T(8,128)S(1)} fusion(bf16[2048,1536]{1,0:T(8,128)(2,1)S(1)} %copy-done.5, pred[2048]{0:T(1024)(128)(4,1)S(1)} %reshape.60, bf16[3,512,1536]{2,1,0:T(8,128)(2,1)} %param.7), kind=kOutput, calls=%fused_computation.3 | convolution fusion | flops 3224371200 | bytes 12060672 | tf_op jit(solution)/shard_map/dot_general | solution.py:22
  69.3 5.2 %add_convert_fusion.1 = bf16[2048,512]{1,0:T(8,128)(2,1)S(1)} fusion(f32[2048,512]{1,0:T(8,128)S(1)} %fusion, f32[2048,512]{1,0:T(8,128)S(1)} %fusion.2, bf16[2048,1536]{1,0:T(8,128)(2,1)S(1)} %copy-done.5, pred[2048]{0:T(1024)(128)(4,1)S(1)} %reshape.58, bf16[3,512,1536]{2,1,0:T(8,128)(2,1)} %param.7), kind=kOutput, calls=%fused_computation.11 | convolution fusion | flops 3227516928 | bytes 18352128 | tf_op jit(solution)/shard_map/dot_general | solution.py:22
  74.5 0.7 fusion.41
  75.2 0.7 fusion.40
  75.9 0.7 fusion.39
  76.6 0.7 fusion.38
  77.4 0.7 fusion.37
  78.1 0.7 fusion.36
  78.8 0.7 fusion.35
  79.5 0.7 fusion.34
  80.2 3.6 %all-to-all-start.1 = ((bf16[8,256,512]{2,1,0:T(8,128)(2,1)}), bf16[8,256,512]{2,1,0:T(8,128)(2,1)S(1)}, u32[]{:S(2)}, u32[]{:S(2)}) async-start(bf16[8,256,512]{2,1,0:T(8,128)(2,1)} %fusion.34), calls=%async_computation.2 | async-start | bytes 4194304 | tf_op jit(solution)/shard_map/all_to_all | solution.py:32
  83.9 22.0 %all-gather.5.cloned.1.call-done = bf16[256,4096]{0,1:T(8,128)(2,1)} async-done(((bf16[256,1024]{0,1:T(8,128)(2,1)}), bf16[256,4096]{0,1:T(8,128)(2,1)}) %all-gather.5.cloned.1.call-update) | async-done | bytes 2097168 | tf_op jit(solution)/shard_map/all_gather | solution.py:17
  105.9 4.5 %all-to-all-done.1 = bf16[8,256,512]{2,1,0:T(8,128)(2,1)S(1)} async-done(((bf16[8,256,512]{2,1,0:T(8,128)(2,1)}), bf16[8,256,512]{2,1,0:T(8,128)(2,1)S(1)}, u32[]{:S(2)}, u32[]{:S(2)}) %all-to-all-start.1) | async-done | bytes 2097184 | tf_op jit(solution)/shard_map/all_to_all | solution.py:32
  110.4 1.3 copy-done.1
  111.7 3.6 %all-to-all-start = ((bf16[256,8,512]{0,2,1:T(8,128)(2,1)}), bf16[256,8,512]{0,2,1:T(8,128)(2,1)S(1)}, u32[]{:S(2)}, u32[]{:S(2)}) async-start(bf16[256,8,512]{0,2,1:T(8,128)(2,1)} %bitcast.98), calls=%async_computation | async-start | bytes 4194304 | tf_op jit(solution)/shard_map/all_to_all | solution.py:18
  115.3 0.0 reduce-scatter.5.cloned.1.call-start
  115.4 3.9 %copy.24 = bf16[256,8,512]{0,2,1:T(8,128)(2,1)} copy(bf16[256,8,512]{2,0,1:T(8,128)(2,1)} %bitcast.97) | data formatting | bytes 4194304 | tf_op jit(solution)/shard_map/reshape | solution.py:31
  119.3 0.0 reduce-scatter.5.cloned.1.call-update
  119.3 0.2 reduce-scatter.3.cloned.1.call-start
  119.6 22.3 %all-to-all-done = bf16[256,8,512]{0,2,1:T(8,128)(2,1)S(1)} async-done(((bf16[256,8,512]{0,2,1:T(8,128)(2,1)}), bf16[256,8,512]{0,2,1:T(8,128)(2,1)S(1)}, u32[]{:S(2)}, u32[]{:S(2)}) %all-to-all-start) | async-done | bytes 2097184 | tf_op jit(solution)/shard_map/all_to_all | solution.py:18
  141.9 2.9 %broadcast_select_fusion = (bf16[8,256,512]{1,2,0:T(8,128)(2,1)}, bf16[8,256,512]{1,2,0:T(8,128)(2,1)}, bf16[8,256,512]{1,2,0:T(8,128)(2,1)}) fusion(pred[8,256]{1,0:T(8,128)(4,1)S(1)} %bitcast.101, bf16[256,8,512]{0,2,1:T(8,128)(2,1)S(1)} %all-to-all-done, pred[8,256]{1,0:T(8,128)(4,1)S(1)} %bitcast.103, pred[8,256]{1,0:T(8,128)(4,1)S(1)} %bitcast.102), kind=kLoop, calls=%fused_computation.27 | loop fusion | flops 3145728 | bytes 8394752 | tf_op jit(solution)/shard_map/jit(_where)/select_n | solution.py:39
  144.8 3.9 %copy.19 = bf16[8,256,512]{2,1,0:T(8,128)(2,1)} copy(bf16[8,256,512]{1,2,0:T(8,128)(2,1)} %get-tuple-element.16) | data formatting | bytes 4194304 | tf_op jit(solution)/shard_map/jit(_where)/select_n | solution.py:39
  148.7 3.9 %copy.21 = bf16[8,256,512]{2,1,0:T(8,128)(2,1)} copy(bf16[8,256,512]{1,2,0:T(8,128)(2,1)} %get-tuple-element.17) | data formatting | bytes 4194304 | tf_op jit(solution)/shard_map/jit(_where)/select_n | solution.py:39
  152.7 3.9 %copy.23 = bf16[8,256,512]{2,1,0:T(8,128)(2,1)} copy(bf16[8,256,512]{1,2,0:T(8,128)(2,1)} %get-tuple-element.15) | data formatting | bytes 4194304 | tf_op jit(solution)/shard_map/jit(_where)/select_n | solution.py:39
  156.6 10.1 %fusion.26 = f32[2048,1536]{1,0:T(8,128)} fusion(bf16[2048,512]{1,0:T(8,128)(2,1)} %bitcast.99, bf16[3,512,1536]{2,1,0:T(8,128)(2,1)} %param.7), kind=kOutput, calls=%fused_computation.36 | convolution fusion | flops 3221225472 | bytes 16252928 | tf_op jit(solution)/shard_map/dot_general | solution.py:38
  166.8 7.9 %fusion.23 = f32[2048,1536]{1,0:T(8,128)} fusion(bf16[2048,512]{1,0:T(8,128)(2,1)S(1)} %bitcast.100, bf16[3,512,1536]{2,1,0:T(8,128)(2,1)} %param.7), kind=kOutput, calls=%fused_computation.33 | convolution fusion | flops 3221225472 | bytes 16252928 | tf_op jit(solution)/shard_map/dot_general | solution.py:38
  174.6 0.0 copy-done
  174.6 13.3 %add_convert_fusion = bf16[2048,1536]{1,0:T(8,128)(2,1)} fusion(f32[2048,1536]{1,0:T(8,128)} %fusion.26, f32[2048,1536]{1,0:T(8,128)} %fusion.23, bf16[2048,512]{1,0:T(8,128)(2,1)S(1)} %bitcast.95, bf16[3,512,1536]{2,1,0:T(8,128)(2,1)} %param.7), kind=kOutput, calls=%fused_computation | convolution fusion | flops 3230662656 | bytes 35127296 | tf_op jit(solution)/shard_map/dot_general | solution.py:38
  187.9 0.0 reduce-scatter.3.cloned.1.call-update
  187.9 2.4 copy.25
  190.3 4.1 %bitcast_select_fusion.2 = (bf16[2048,512]{1,0:T(8,128)(2,1)S(1)}, bf16[2048,512]{1,0:T(8,128)(2,1)S(1)}, bf16[2048,512]{1,0:T(8,128)(2,1)S(1)}) fusion(bf16[8,256,512]{2,1,0:T(8,128)(2,1)} %copy.25, pred[2048]{0:T(1024)(128)(4,1)S(1)} %reshape.58, pred[2048]{0:T(1024)(128)(4,1)S(1)} %reshape.60, pred[2048]{0:T(1024)(128)(4,1)S(1)} %reshape.62), kind=kLoop, calls=%fused_computation.26 | loop fusion | flops 3145728 | bytes 8394752 | tf_op jit(solution)/shard_map/jit(_where)/select_n | solution.py:39
  194.4 0.0 slice-start.1
  194.4 7.4 %fusion.15 = bf16[1,512,1536]{2,1,0:T(8,128)(2,1)S(1)} fusion(bf16[2048,512]{1,0:T(8,128)(2,1)S(1)} %get-tuple-element.14, bf16[2048,1536]{1,0:T(8,128)(2,1)} %all-gather.7.cloned.1.call-done), kind=kOutput, calls=%fused_computation.21 | convolution fusion | flops 3222798336 | bytes 9961472 | tf_op jit(solution)/shard_map/dot_general | solution.py:50
  201.8 3.6 %fusion.16 = bf16[1,512,1536]{2,1,0:T(8,128)(2,1)S(1)} fusion(bf16[2048,512]{1,0:T(8,128)(2,1)S(1)} %get-tuple-element.13, bf16[2048,1536]{1,0:T(8,128)(2,1)S(1)} %bitcast.106), kind=kOutput, calls=%fused_computation.22 | convolution fusion | flops 3222798336 | bytes 9961472 | tf_op jit(solution)/shard_map/dot_general | solution.py:50
  205.4 3.6 %fusion.17 = bf16[1,512,1536]{2,1,0:T(8,128)(2,1)S(1)} fusion(bf16[2048,512]{1,0:T(8,128)(2,1)S(1)} %get-tuple-element.12, bf16[2048,1536]{1,0:T(8,128)(2,1)S(1)} %bitcast.106), kind=kOutput, calls=%fused_computation.23 | convolution fusion | flops 3222798336 | bytes 9961472 | tf_op jit(solution)/shard_map/dot_general | solution.py:50
  209.0 2.5 pad_maximum_fusion
  211.5 2.2 copy.26
  213.7 35.2 %reduce-scatter.3.cloned.1.call-done = bf16[256,1536]{1,0:T(8,128)(2,1)} async-done(((bf16[2048,1536]{1,0:T(8,128)(2,1)}), bf16[256,1536]{1,0:T(8,128)(2,1)}) %reduce-scatter.3.cloned.1.call-update) | async-done | bytes 786448 | tf_op jit(solution)/shard_map/reduce_scatter | solution.py:46
  (19 shorter events, 0.1 us)
Async XLA Ops:
  7.2 2.9 %copy-start.3 = (s32[8]{0:T(128)S(1)}, s32[8]{0:T(128)}, u32[]{:S(2)}) copy-start(s32[8]{0:T(128)} %param.9) | copy-start | bytes 100
  7.2 3.6 %copy-start.4 = (s32[256]{0:T(256)S(1)}, s32[256]{0:T(256)}, u32[]{:S(2)}) copy-start(s32[256]{0:T(256)} %param.8) | copy-start | bytes 3076
  7.2 50.8 %all-gather.7.cloned.1.call-start = ((), (), s32[]{:S(2)}) async-start(), calls=%async_computation.6 | async-start | bytes 7077888 | tf_op jit(solution)/shard_map/all_gather | solution.py:16
  7.9 97.9 %all-gather.5.cloned.1.call-start = ((), (), s32[]{:S(2)}) async-start(), calls=%async_computation.4 | async-start | bytes 2621440 | tf_op jit(solution)/shard_map/all_gather | solution.py:17
  58.0 6.3 %copy-start.5 = (bf16[2048,1536]{1,0:T(8,128)(2,1)S(1)}, bf16[2048,1536]{1,0:T(8,128)(2,1)}, u32[]{:S(2)}) copy-start(bf16[2048,1536]{1,0:T(8,128)(2,1)} %all-gather.7.cloned.1.call-done) | copy-start | bytes 18874372
  80.2 30.2 %all-to-all-start.1 = ((bf16[8,256,512]{2,1,0:T(8,128)(2,1)}), bf16[8,256,512]{2,1,0:T(8,128)(2,1)S(1)}, u32[]{:S(2)}, u32[]{:S(2)}) async-start(bf16[8,256,512]{2,1,0:T(8,128)(2,1)} %fusion.34), calls=%async_computation.2 | async-start | bytes 4194304 | tf_op jit(solution)/shard_map/all_to_all | solution.py:32
  110.4 1.3 copy-start.1
  111.7 30.2 %all-to-all-start = ((bf16[256,8,512]{0,2,1:T(8,128)(2,1)}), bf16[256,8,512]{0,2,1:T(8,128)(2,1)S(1)}, u32[]{:S(2)}, u32[]{:S(2)}) async-start(bf16[256,8,512]{0,2,1:T(8,128)(2,1)} %bitcast.98), calls=%async_computation | async-start | bytes 4194304 | tf_op jit(solution)/shard_map/all_to_all | solution.py:18
  115.3 96.2 %reduce-scatter.5.cloned.1.call-start = ((), (), s32[]{:S(2)}) async-start(), calls=%async_computation.7 | async-start | bytes 2621440 | tf_op jit(solution)/shard_map/reduce_scatter | solution.py:35
  119.3 129.6 %reduce-scatter.3.cloned.1.call-start = ((), (), s32[]{:S(2)}) async-start(), calls=%async_computation.5 | async-start | bytes 7077888 | tf_op jit(solution)/shard_map/reduce_scatter | solution.py:46
  156.6 10.1 %copy-start.2 = (bf16[8,256,512]{2,1,0:T(8,128)(2,1)S(1)}, bf16[8,256,512]{2,1,0:T(8,128)(2,1)}, u32[]{:S(2)}) copy-start(bf16[8,256,512]{2,1,0:T(8,128)(2,1)} %copy.21) | copy-start | bytes 6291460
  166.8 7.9 %copy-start = (bf16[8,256,512]{2,1,0:T(8,128)(2,1)S(1)}, bf16[8,256,512]{2,1,0:T(8,128)(2,1)}, u32[]{:S(2)}) copy-start(bf16[8,256,512]{2,1,0:T(8,128)(2,1)} %copy.23) | copy-start | bytes 6291460
  190.3 11.5 %slice-start = ((s8[6291456]{0:T(1024)(128)(4,1)}), s8[4194304]{0:T(1024)(128)(4,1)S(1)}, s32[]{:S(2)}) async-start(s8[6291456]{0:T(1024)(128)(4,1)} %bitcast.105), calls=%async_computation.8 | async-start | bytes 8388608
  194.4 7.4 %slice-start.1 = ((s8[6291456]{0:T(1024)(128)(4,1)}), s8[2097152]{0:T(1024)(128)(4,1)S(1)}, s32[]{:S(2)}) async-start(s8[6291456]{0:T(1024)(128)(4,1)} %bitcast.105), calls=%async_computation.9 | async-start | bytes 4194304
Sparse Core Ops, SparseCore 0:
  9.9 48.1 all-gather.6
  60.2 45.6 all-gather.4
  119.5 44.9 reduce-scatter.4
  188.1 60.8 reduce-scatter.2
